TPU v7x, 512 devices: a whole 4x8x8 slice. The times are simulated.
512 devices in a mesh: dom: 64 (over z, x, core), col: 8 (over y).
Axes of the slice: x: 4, y: 8, z: 8, core: 2. Of those that a mesh axis runs over, the one named last changes fastest.
Arguments:
- feature: bfloat16 [32768, 1024], P('dom', 'col'), may hold values from -6 to 6
- cotangent: bfloat16 [32768, 1024], P('dom', 'col'), may hold values from -6 to 6
- node_type: int32 [32768], P('dom'), may hold values from 0 to 2
- self_gain: float32 [3, 1024], P(None, 'col'), may hold values from 0.1 to 1.9
- weights: bfloat16 [8, 1024, 1024], P(None, 'dom', 'col'), may hold values from -0.1875 to 0.1875
- tile_values: bfloat16 [2048, 128, 128], P('dom'), may hold values from -0.5 to 0.5
- tile_rel: int32 [2048], P('dom'), may hold values from 0 to 7
- tile_src: int32 [2048], P('dom'), may hold values from 0 to 3
- tile_peer: int32 [2048], P('dom'), may hold values from 0 to 63, as said below
- tile_count: int32 [64], P('dom'), may hold values from 24 to 32, as said below
- send_block: int32 [64, 64], P('dom'), may hold values from -1 to 3, as said below
Outputs:
- feature_grad: bfloat16 [32768, 1024], P('dom', 'col')
- weight_grad: bfloat16 [8, 1024, 1024], P(None, None, 'col')
Inputs may be any that keep to these rules, and one draw needn't show every extreme that they name: Slots 0 to tile_count - 1 of each partition hold its tiles, the others hold none; some partition uses all 32 slots in every draw. `tile_peer`: the used slots of one partition name distinct owner partitions. send_block[o, p] is at least 0 exactly when some used slot of partition p names o, and then it is that slot's destination block within o.
All inputs are finite; a program needn't handle non-finite values.
Results may differ from a plain program's by a relative error of at most 0.0052.
Values may be sent and summed in bfloat16 or wider, within the bound.
No kernel may reach another device: no remote copies, remote signals or barrier semaphores. Data moves between devices by JAX's collectives and lax.ppermute only.
A program may use at most 64 MiB of HBM per device.

v0:
```python
import math
import jax
import jax.numpy as jnp
from jax import lax
from jax.sharding import PartitionSpec as P


def body(
    feature,
    cotangent,
    node_type,
    self_gain,
    weights,
    tile_values,
    tile_rel,
    tile_src,
    tile_peer,
    tile_count,
    send_block,
):
    partitions = lax.axis_size("dom")
    row_count, col_width = cotangent.shape
    tile_size = tile_values.shape[1]
    block_count = row_count // tile_size
    relations = weights.shape[0]
    slot_count = tile_values.shape[0]
    type_count = self_gain.shape[0]
    grad_blocks = cotangent.reshape(block_count, tile_size, col_width)
    wanted = send_block[0]
    chooser = (wanted[:, None] == jnp.arange(block_count, dtype=jnp.int32)[None, :]).astype(
        jnp.bfloat16
    )
    outgoing = jnp.einsum(
        "pb,btk->ptk", chooser, grad_blocks, preferred_element_type=jnp.float32
    ).astype(jnp.bfloat16)
    incoming = lax.all_to_all(outgoing, "dom", split_axis=0, concat_axis=0, tiled=True)
    picked = jnp.take(incoming, tile_peer, axis=0)
    contribs = jnp.einsum("tds,tdk->tsk", tile_values, picked, preferred_element_type=jnp.float32)
    is_used = jnp.arange(slot_count, dtype=jnp.int32) < tile_count[0]
    slot_of = tile_rel * block_count + tile_src
    slot_table = (
        (slot_of[None, :] == jnp.arange(relations * block_count, dtype=jnp.int32)[:, None])
        & is_used[None, :]
    ).astype(jnp.float32)
    merged = jnp.einsum("mt,tsk->msk", slot_table, contribs, precision=lax.Precision.HIGHEST)
    block_grad = merged.astype(jnp.bfloat16).reshape(relations, row_count, col_width)
    kind_table = (node_type[:, None] == jnp.arange(type_count, dtype=jnp.int32)[None, :]).astype(
        jnp.float32
    )
    self_gains = jnp.dot(kind_table, self_gain, precision=lax.Precision.HIGHEST)
    self_term = cotangent.astype(jnp.float32) * self_gains
    weight_full = lax.all_gather(weights, "dom", axis=1, tiled=True)
    weight_cols = lax.all_to_all(weight_full, "col", split_axis=1, concat_axis=2, tiled=True)
    aggregated = jnp.einsum(
        "rnk,rjk->nj",
        lax.all_gather(block_grad, "col", axis=2, tiled=True),
        weight_cols,
        preferred_element_type=jnp.float32,
    )
    feature_grad = (aggregated + self_term).astype(jnp.bfloat16)
    weight_terms = jnp.einsum(
        "nj,rnk->rjk",
        lax.all_gather(feature, "col", axis=1, tiled=True),
        block_grad,
        preferred_element_type=jnp.float32,
    )
    norm_scale = 1.0 / math.sqrt(row_count * partitions)
    summed = lax.psum(weight_terms, "dom")
    weight_grad = (summed * norm_scale).astype(jnp.bfloat16)
    return (feature_grad, weight_grad)


def solution(mesh):
    return jax.shard_map(
        body,
        mesh=mesh,
        in_specs=(
            P("dom", "col"),
            P("dom", "col"),
            P("dom"),
            P(None, "col"),
            P(None, "dom", "col"),
            P("dom", None, None),
            P("dom"),
            P("dom"),
            P("dom"),
            P("dom"),
            P("dom", None),
        ),
        out_specs=(P("dom", "col"), P(None, None, "col")),
        check_vma=False,
    )
```

profile of v0, /device:TPU:2, one launch (start us, length us, event | category | flops | bytes accessed | tf_op | source)
XLA Modules:
  0.0 470.0 jit_solution(14236573666321858946)
XLA Ops:
  7.2 0.0 copy-start
  7.2 0.0 all-gather.8.cloned.1.call-start
  7.2 0.7 all-gather.8.cloned.1.call-update
  7.9 1.7 convolution_convert_fusion
  9.6 2.7 copy.38
  12.3 14.0 %all-to-all-start = ((bf16[64,128,128]{2,1,0:T(8,128)(2,1)}), bf16[64,128,128]{2,1,0:T(8,128)(2,1)S(1)}, u32[]{:S(2)}, u32[]{:S(2)}) async-start(bf16[64,128,128]{2,1,0:T(8,128)(2,1)} %copy.38), calls=%async_computation | async-start | bytes 4194304 | tf_op jit(solution)/shard_map/all_to_all | solution.py:36
  26.3 0.0 all-gather.6.cloned.1.call-start
  26.4 0.6 copy.42
  27.0 0.1 all-gather.6.cloned.1.call-update
  27.1 0.0 all-reduce.2.cloned.1.call-start
  27.8 49.7 %all-to-all-done = bf16[64,128,128]{2,1,0:T(8,128)(2,1)S(1)} async-done(((bf16[64,128,128]{2,1,0:T(8,128)(2,1)}), bf16[64,128,128]{2,1,0:T(8,128)(2,1)S(1)}, u32[]{:S(2)}, u32[]{:S(2)}) %all-to-all-start) | async-done | bytes 2097184 | tf_op jit(solution)/shard_map/all_to_all | solution.py:36
  77.6 1.7 gather_fusion
  79.3 3.1 convolution_bitcast_fusion.1
  82.4 2.4 copy.40
  84.8 1.1 convolution_convert_fusion.1
  85.9 0.4 copy.41
  86.3 0.0 all-gather.8.cloned.1.call-done
  86.4 4.8 %convolution_bitcast_fusion = f32[8,1024,128]{1,2,0:T(8,128)} fusion(bf16[8,512,128]{2,1,0:T(8,128)(2,1)S(1)} %bitcast.32, bf16[512,1024]{1,0:T(8,128)(2,1)} %all-gather.8.cloned.1.call-done), kind=kOutput, calls=%fused_computation.2 | convolution fusion | flops 1073741824 | bytes 6291456 | tf_op jit(solution)/shard_map/nj,rnk->rjk/dot_general | solution.py:61
  91.2 0.0 all-reduce.2.cloned.1.call-update
  91.2 0.0 all-gather.4.cloned.1.call-start
  91.3 0.5 all-gather.4.cloned.1.call-update
  91.8 50.8 %all-gather.6.cloned.1.call-done = bf16[8,1024,128]{2,0,1:T(8,128)(2,1)} async-done(((bf16[8,16,128]{2,0,1:T(8,128)(2,1)}), bf16[8,1024,128]{2,0,1:T(8,128)(2,1)}) %all-gather.6.cloned.1.call-update) | async-done | bytes 2097168 | tf_op jit(solution)/shard_map/all_gather | solution.py:52
  142.7 6.7 %all-to-all-start.1 = ((bf16[8,1024,128]{2,0,1:T(8,128)(2,1)}), bf16[8,1024,128]{2,0,1:T(8,128)(2,1)}, u32[]{:S(2)}, u32[]{:S(2)}) async-start(bf16[8,1024,128]{2,0,1:T(8,128)(2,1)} %all-gather.6.cloned.1.call-done), calls=%async_computation.1 | async-start | bytes 4194304 | tf_op jit(solution)/shard_map/all_to_all | solution.py:53
  149.4 202.8 %all-reduce.2.cloned.1.call-done = f32[8,1024,128]{1,2,0:T(8,128)} async-done(((f32[8,1024,128]{1,2,0:T(8,128)}), f32[8,1024,128]{1,2,0:T(8,128)}) %all-reduce.2.cloned.1.call-update) | async-done | bytes 4194320 | tf_op jit(solution)/shard_map/psum | solution.py:68
  352.2 2.8 multiply_convert_fusion
  355.0 2.4 copy.45
  357.4 0.0 all-to-all-done.1
  357.4 2.9 copy.51
  360.3 2.4 all_to_all.20
  362.7 93.4 %all-gather.4.cloned.1.call-done = bf16[8,512,1024]{2,1,0:T(8,128)(2,1)} async-done(((bf16[8,512,128]{2,1,0:T(8,128)(2,1)}), bf16[8,512,1024]{2,1,0:T(8,128)(2,1)}) %all-gather.4.cloned.1.call-update) | async-done | bytes 8388624 | tf_op jit(solution)/shard_map/all_gather | solution.py:56
  456.2 6.3 %convolution_bitcast_fusion.2 = f32[512,128]{1,0:T(8,128)S(1)} fusion(bf16[8,512,1024]{2,1,0:T(8,128)(2,1)} %all-gather.4.cloned.1.call-done, bf16[8,128,1024]{2,1,0:T(8,128)(2,1)} %all_to_all.20), kind=kOutput, calls=%fused_computation.9 | convolution fusion | flops 1073741824 | bytes 10747904 | tf_op jit(solution)/shard_map/rnk,rjk->nj/dot_general | solution.py:54
  462.5 1.0 fusion.1
  (22 shorter events, 0.1 us)
Async XLA Ops:
  7.2 72.1 %copy-start = (bf16[32,128,128]{2,1,0:T(8,128)(2,1)S(1)}, bf16[32,128,128]{2,1,0:T(8,128)(2,1)}, u32[]{:S(2)}) copy-start(bf16[32,128,128]{2,1,0:T(8,128)(2,1)} %param.16) | copy-start | bytes 3145732
  7.2 79.2 %all-gather.8.cloned.1.call-start = ((), (), s32[]{:S(2)}) async-start(), calls=%async_computation.4 | async-start | bytes 1179648 | tf_op jit(solution)/shard_map/all_gather | solution.py:63
  12.3 14.1 %copy-start.3 = (bf16[8,16,128]{2,1,0:T(8,128)(2,1)S(1)}, bf16[8,16,128]{2,1,0:T(8,128)(2,1)}, u32[]{:S(2)}) copy-start(bf16[8,16,128]{2,1,0:T(8,128)(2,1)} %param.15) | copy-start | bytes 98308
  12.3 15.5 %copy-start.6 = (s32[32]{0:T(128)S(1)}, s32[32]{0:T(128)}, u32[]{:S(2)}) copy-start(s32[32]{0:T(128)} %param.19) | copy-start | bytes 388
  12.3 15.5 %copy-start.7 = (s32[32]{0:T(128)S(1)}, s32[32]{0:T(128)}, u32[]{:S(2)}) copy-start(s32[32]{0:T(128)} %param.18) | copy-start | bytes 388
  12.3 15.5 %copy-start.8 = (s32[32]{0:T(128)S(1)}, s32[32]{0:T(128)}, u32[]{:S(2)}) copy-start(s32[32]{0:T(128)} %param.17) | copy-start | bytes 388
  12.3 65.3 %all-to-all-start = ((bf16[64,128,128]{2,1,0:T(8,128)(2,1)}), bf16[64,128,128]{2,1,0:T(8,128)(2,1)S(1)}, u32[]{:S(2)}, u32[]{:S(2)}) async-start(bf16[64,128,128]{2,1,0:T(8,128)(2,1)} %copy.38), calls=%async_computation | async-start | bytes 4194304 | tf_op jit(solution)/shard_map/all_to_all | solution.py:36
  26.3 116.4 %all-gather.6.cloned.1.call-start = ((), (), s32[]{:S(2)}) async-start(), calls=%async_computation.3 | async-start | bytes 2129920 | tf_op jit(solution)/shard_map/all_gather | solution.py:52
  27.1 325.2 %all-reduce.2.cloned.1.call-start = ((), (), s32[]{:S(2)}) async-start(), calls=%async_computation.5 | async-start | bytes 8388608 | tf_op jit(solution)/shard_map/psum | solution.py:68
  86.3 4.9 %copy-start.1 = (bf16[32,128,128]{2,1,0:T(8,128)(2,1)}, bf16[32,128,128]{2,1,0:T(8,128)(2,1)S(1)}, u32[]{:S(2)}) copy-start(bf16[32,128,128]{2,1,0:T(8,128)(2,1)S(1)} %copy.41) | copy-start | bytes 3145732
  91.2 364.9 %all-gather.4.cloned.1.call-start = ((), (), s32[]{:S(2)}) async-start(), calls=%async_computation.2 | async-start | bytes 9437184 | tf_op jit(solution)/shard_map/all_gather | solution.py:56
  142.7 214.7 %all-to-all-start.1 = ((bf16[8,1024,128]{2,0,1:T(8,128)(2,1)}), bf16[8,1024,128]{2,0,1:T(8,128)(2,1)}, u32[]{:S(2)}, u32[]{:S(2)}) async-start(bf16[8,1024,128]{2,0,1:T(8,128)(2,1)} %all-gather.6.cloned.1.call-done), calls=%async_computation.1 | async-start | bytes 4194304 | tf_op jit(solution)/shard_map/all_to_all | solution.py:53
  362.7 99.8 %copy-start.2 = (bf16[512,128]{1,0:T(8,128)(2,1)S(1)}, bf16[512,128]{1,0:T(8,128)(2,1)}, u32[]{:S(2)}) copy-start(bf16[512,128]{1,0:T(8,128)(2,1)} %param.12) | copy-start | bytes 393220
  362.7 99.8 %copy-start.4 = (f32[3,128]{1,0:T(4,128)S(1)}, f32[3,128]{1,0:T(4,128)}, u32[]{:S(2)}) copy-start(f32[3,128]{1,0:T(4,128)} %param.14) | copy-start | bytes 4612
  362.7 99.8 %copy-start.5 = (s32[512]{0:T(512)S(1)}, s32[512]{0:T(512)}, u32[]{:S(2)}) copy-start(s32[512]{0:T(512)} %param.13) | copy-start | bytes 6148
Sparse Core Ops, SparseCore 0:
  10.0 46.7 all-gather.7
  60.7 81.9 all-gather.5
  146.2 205.9 all-reduce.1
  354.3 101.8 all-gather.3
where the time goes:
time: 471 us; the launch traced here: 470 us
  waiting for transfers between devices  398 us (85%)
  starting transfers between devices  20.9 us (4%)
  matrix products  18.1 us (4%)
  local copies, waits for them, and re-layouts  15.5 us (3%)
  between operations  14.6 us (3%)
    psum x1, waiting for transfers between devices, body(): summed = lax.psum(weight_terms, 'dom')  203 us
    all_gather x1, waiting for transfers between devices, body(): lax.all_gather(block_grad, 'col', axis=2, tiled=True)  93.4 us
    all_gather x1, waiting for transfers between devices, body(): weight_full = lax.all_gather(weights, 'dom', axis=1, tiled=True)  50.8 us
    all_to_all x1, waiting for transfers between devices, body(): lax.all_to_all(outgoing, 'dom', split_axis=0, concat_axis=0, tiled=True)  49.7 us
    all_to_all x1, starting transfers between devices, body(): lax.all_to_all(outgoing, 'dom', split_axis=0, concat_axis=0, tiled=True)  14 us
  transfers between devices with their start and end apart: 6, of which 4 were waited for; matrix products, arithmetic and copies ran while one was open for 6% of the time, Pallas kernels for 0%

commit v1 on v0

--- a/solution.py
+++ b/solution.py
@@ -3,6 +3,22 @@
 import jax.numpy as jnp
 from jax import lax
 from jax.sharding import PartitionSpec as P
+
+
+def product_in_turn(shard, axis, dim, term):
+    size, place, extent = (lax.axis_size(axis), lax.axis_index(axis), shard.shape[dim])
+    right = [(i, (i + 1) % size) for i in range(size)]
+    left = [(i, (i - 1) % size) for i in range(size)]
+    halfway = size // 2
+    from_left = from_right = shard
+    running = term(shard, place * extent)
+    for step in range(1, halfway + 1):
+        from_left = lax.ppermute(from_left, axis, right)
+        if step < size - halfway:
+            from_right = lax.ppermute(from_right, axis, left)
+            running = running + term(from_right, (place + step) % size * extent)
+        running = running + term(from_left, (place - step) % size * extent)
+    return running
 
 
 def body(
@@ -51,11 +67,16 @@
     self_term = cotangent.astype(jnp.float32) * self_gains
     weight_full = lax.all_gather(weights, "dom", axis=1, tiled=True)
     weight_cols = lax.all_to_all(weight_full, "col", split_axis=1, concat_axis=2, tiled=True)
-    aggregated = jnp.einsum(
-        "rnk,rjk->nj",
-        lax.all_gather(block_grad, "col", axis=2, tiled=True),
-        weight_cols,
-        preferred_element_type=jnp.float32,
+    aggregated = product_in_turn(
+        block_grad,
+        "col",
+        2,
+        lambda shard, offset: jnp.einsum(
+            "rnk,rjk->nj",
+            shard,
+            lax.dynamic_slice_in_dim(weight_cols, offset, shard.shape[2], axis=2),
+            preferred_element_type=jnp.float32,
+        ),
     )
     feature_grad = (aggregated + self_term).astype(jnp.bfloat16)
     weight_terms = jnp.einsum(

time: 471 us -> 438 us (0.930)
  waiting for transfers between devices: 398 us -> 326 us
  starting transfers between devices: 20.9 us -> 45.6 us
  local copies, waits for them, and re-layouts: 15.5 us -> 22.4 us
  matrix products: 18.1 us -> 23.9 us
    all_gather x1 -> x0, waiting for transfers between devices: 93.4 us -> none  [body(): lax.all_gather(block_grad, 'col', axis=2, tiled=True)]
    all_gather x1, waiting for transfers between devices: 0.02 us -> 50.7 us  [body(): lax.all_gather(feature, 'col', axis=1, tiled=True)]
    all_to_all x1, waiting for transfers between devices: 49.7 us -> 0.01 us  [body(): lax.all_to_all(outgoing, 'dom', split_axis=0, concat_axis=0, tiled=True)]
    psum x1, waiting for transfers between devices: 203 us -> 167 us  [body(): summed = lax.psum(weight_terms, 'dom')]
    ppermute x0 -> x7, waiting for transfers between devices: none -> 33 us  [the longest x4 17.7 us: product_in_turn(): from_left = lax.ppermute(from_left, axis, right)]
    ppermute x0 -> x7, starting transfers between devices: none -> 24.4 us  [the longest x3 14.6 us: product_in_turn(): from_right = lax.ppermute(from_right, axis, left)]
    all_gather x1, waiting for transfers between devices: 50.8 us -> 74.6 us  [body(): weight_full = lax.all_gather(weights, 'dom', axis=1, tiled=True)]
    dot_general x1 -> x8, matrix products: 6.31 us -> 12.7 us  [body(): jnp.einsum('rnk,rjk->nj', shard, lax.dynamic_slice_in_dim(weight_cols, of...]
  transfers between devices with their start and end apart: 6 -> 12, of which waited for: 4 -> 8; matrix products, arithmetic and copies ran while one was open for 6% -> 10% of each run, Pallas kernels for 0% -> 0%
where the time goes in v1:
time: 438 us; the launch traced here: 437 us
  waiting for transfers between devices  326 us (74%)
  starting transfers between devices  45.6 us (10%)
  matrix products  23.9 us (5%)
  local copies, waits for them, and re-layouts  22.4 us (5%)
  between operations  14.8 us (3%)
    psum x1, waiting for transfers between devices, body(): summed = lax.psum(weight_terms, 'dom')  167 us
    all_gather x1, waiting for transfers between devices, body(): weight_full = lax.all_gather(weights, 'dom', axis=1, tiled=True)  74.6 us
    all_gather x1, waiting for transfers between devices, body(): lax.all_gather(feature, 'col', axis=1, tiled=True)  50.7 us
    ppermute x4, waiting for transfers between devices, product_in_turn(): from_left = lax.ppermute(from_left, axis, right)  17.7 us
    ppermute x3, waiting for transfers between devices, product_in_turn(): from_right = lax.ppermute(from_right, axis, left)  15.3 us
    ppermute x3, starting transfers between devices, product_in_turn(): from_right = lax.ppermute(from_right, axis, left)  14.6 us
    all_to_all x1, starting transfers between devices, body(): lax.all_to_all(outgoing, 'dom', split_axis=0, concat_axis=0, tiled=True)  14.2 us
    dot_general x8, matrix products, body(): jnp.einsum('rnk,rjk->nj', shard, lax.dynamic_slice_in_dim(weight_cols, of...  12.7 us
  transfers between devices with their start and end apart: 12, of which 8 were waited for; matrix products, arithmetic and copies ran while one was open for 10% of the time, Pallas kernels for 0%

profile of v1, /device:TPU:2, one launch (start us, length us, event | category | flops | bytes accessed | tf_op | source)
XLA Modules:
  0.0 437.1 jit_solution(5671091883188988174)
XLA Ops:
  8.7 1.7 convolution_convert_fusion
  10.4 2.7 copy.38
  13.1 14.2 %all-to-all-start = ((bf16[64,128,128]{2,1,0:T(8,128)(2,1)}), bf16[64,128,128]{2,1,0:T(8,128)(2,1)}, u32[]{:S(2)}, u32[]{:S(2)}) async-start(bf16[64,128,128]{2,1,0:T(8,128)(2,1)} %copy.38), calls=%async_computation | async-start | bytes 4194304 | tf_op jit(solution)/shard_map/all_to_all | solution.py:52
  28.8 74.6 %all-gather.3.cloned.1.call-done = bf16[8,1024,128]{2,0,1:T(8,128)(2,1)} async-done(((bf16[8,16,128]{2,0,1:T(8,128)(2,1)}), bf16[8,1024,128]{2,0,1:T(8,128)(2,1)}) %all-gather.3.cloned.1.call-update) | async-done | bytes 2097168 | tf_op jit(solution)/shard_map/all_gather | solution.py:68
  103.4 6.9 %all-to-all-start.1 = ((bf16[8,1024,128]{2,0,1:T(8,128)(2,1)}), bf16[8,1024,128]{2,0,1:T(8,128)(2,1)}, u32[]{:S(2)}, u32[]{:S(2)}) async-start(bf16[8,1024,128]{2,0,1:T(8,128)(2,1)} %all-gather.3.cloned.1.call-done), calls=%async_computation.1 | async-start | bytes 4194304 | tf_op jit(solution)/shard_map/all_to_all | solution.py:69
  110.3 2.3 gather_fusion
  112.7 1.9 convolution_bitcast_fusion.1
  114.6 3.1 copy.40
  117.7 2.7 convolution_convert_fusion.1
  120.8 3.9 collective-permute-start.1
  124.7 50.7 %all-gather.5.cloned.1.call-done = bf16[512,1024]{1,0:T(8,128)(2,1)} async-done(((bf16[512,128]{1,0:T(8,128)(2,1)}), bf16[512,1024]{1,0:T(8,128)(2,1)}) %all-gather.5.cloned.1.call-update) | async-done | bytes 1048592 | tf_op jit(solution)/shard_map/all_gather | solution.py:84
  175.4 4.5 %convolution_bitcast_fusion = f32[8,1024,128]{1,2,0:T(8,128)} fusion(bf16[8,512,128]{2,1,0:T(8,128)(2,1)S(1)} %bitcast.71, bf16[512,1024]{1,0:T(8,128)(2,1)} %all-gather.5.cloned.1.call-done), kind=kOutput, calls=%fused_computation.2 | convolution fusion | flops 1073741824 | bytes 6291456 | tf_op jit(solution)/shard_map/nj,rnk->rjk/dot_general | solution.py:82
  180.0 4.3 collective-permute-start
  184.3 7.3 %collective-permute-done.1 = bf16[8,512,128]{2,1,0:T(8,128)(2,1)} collective-permute-done((bf16[8,512,128]{2,1,0:T(8,128)(2,1)S(1)}, bf16[8,512,128]{2,1,0:T(8,128)(2,1)}, u32[]{:S(2)}, u32[]{:S(2)}) %collective-permute-start.1) | collective-permute-done | bytes 1048608 | tf_op jit(solution)/shard_map/ppermute | solution.py:16
  191.6 1.9 collective-permute-start.3
  193.5 13.4 %collective-permute-done = bf16[8,512,128]{2,1,0:T(8,128)(2,1)S(1)} collective-permute-done((bf16[8,512,128]{2,1,0:T(8,128)(2,1)S(1)}, bf16[8,512,128]{2,1,0:T(8,128)(2,1)S(1)}, u32[]{:S(2)}, u32[]{:S(2)}) %collective-permute-start) | collective-permute-done | bytes 1048608 | tf_op jit(solution)/shard_map/ppermute | solution.py:18
  206.9 5.6 %collective-permute-start.2 = (bf16[8,512,128]{2,1,0:T(8,128)(2,1)S(1)}, bf16[8,512,128]{2,1,0:T(8,128)(2,1)}, u32[]{:S(2)}, u32[]{:S(2)}) collective-permute-start(bf16[8,512,128]{2,1,0:T(8,128)(2,1)S(1)} %collective-permute-done), channel_id=1, source_target_pairs={{0,7},{1,0},{2,1},{3,2},{4,3},{5,4},{6,5},{7,6},{8,15},{9,8},{10,9... | collective-permute-start | bytes 3145736 | tf_op jit(solution)/shard_map/ppermute | solution.py:18
  212.5 6.7 %collective-permute-done.3 = bf16[8,512,128]{2,1,0:T(8,128)(2,1)} collective-permute-done((bf16[8,512,128]{2,1,0:T(8,128)(2,1)}, bf16[8,512,128]{2,1,0:T(8,128)(2,1)}, u32[]{:S(2)}, u32[]{:S(2)}) %collective-permute-start.3) | collective-permute-done | bytes 1048608 | tf_op jit(solution)/shard_map/ppermute | solution.py:16
  219.2 1.9 collective-permute-start.5
  221.6 167.2 %all-reduce.2.cloned.1.call-done = f32[8,1024,128]{1,2,0:T(8,128)} async-done(((f32[8,1024,128]{1,2,0:T(8,128)}), f32[8,1024,128]{1,2,0:T(8,128)}) %all-reduce.2.cloned.1.call-update) | async-done | bytes 4194320 | tf_op jit(solution)/shard_map/psum | solution.py:89
  388.9 4.1 multiply_convert_fusion
  393.0 3.9 copy.45
  396.9 4.7 %collective-permute-start.4 = (bf16[8,512,128]{2,1,0:T(8,128)(2,1)}, bf16[8,512,128]{2,1,0:T(8,128)(2,1)}, u32[]{:S(2)}, u32[]{:S(2)}) collective-permute-start(bf16[8,512,128]{2,1,0:T(8,128)(2,1)} %collective-permute-done.2), channel_id=1, source_target_pairs={{0,7},{1,0},{2,1},{3,2},{4,3},{5,4},{6,5},{7,6},{8,15},{9,8},{10,9... | collective-permute-start | bytes 3145736 | tf_op jit(solution)/shard_map/ppermute | solution.py:18
  401.6 2.1 collective-permute-start.6
  403.8 4.3 copy.51
  408.0 4.1 all_to_all.20
  413.7 1.7 convolution_bitcast_fusion.7
  417.1 1.7 convolution_bitcast_fusion.3
  419.3 1.7 fusion.3
  421.0 1.9 collective-permute-done.4
  424.6 3.7 collective-permute-done.6
  428.2 2.3 fusion.8
  (38 shorter events, 8.5 us)
Async XLA Ops:
  7.2 105.5 %copy-start = (bf16[32,128,128]{2,1,0:T(8,128)(2,1)S(1)}, bf16[32,128,128]{2,1,0:T(8,128)(2,1)}, u32[]{:S(2)}) copy-start(bf16[32,128,128]{2,1,0:T(8,128)(2,1)} %param.16) | copy-start | bytes 3145732
  7.2 96.2 %all-gather.3.cloned.1.call-start = ((), (), s32[]{:S(2)}) async-start(), calls=%async_computation.2 | async-start | bytes 2129920 | tf_op jit(solution)/shard_map/all_gather | solution.py:68
  13.1 15.6 %copy-start.5 = (s32[32]{0:T(128)S(1)}, s32[32]{0:T(128)}, u32[]{:S(2)}) copy-start(s32[32]{0:T(128)} %param.19) | copy-start | bytes 388
  13.1 15.7 %copy-start.6 = (s32[32]{0:T(128)S(1)}, s32[32]{0:T(128)}, u32[]{:S(2)}) copy-start(s32[32]{0:T(128)} %param.18) | copy-start | bytes 388
  13.1 15.7 %copy-start.7 = (s32[32]{0:T(128)S(1)}, s32[32]{0:T(128)}, u32[]{:S(2)}) copy-start(s32[32]{0:T(128)} %param.17) | copy-start | bytes 388
  13.1 90.3 %all-to-all-start = ((bf16[64,128,128]{2,1,0:T(8,128)(2,1)}), bf16[64,128,128]{2,1,0:T(8,128)(2,1)}, u32[]{:S(2)}, u32[]{:S(2)}) async-start(bf16[64,128,128]{2,1,0:T(8,128)(2,1)} %copy.38), calls=%async_computation | async-start | bytes 4194304 | tf_op jit(solution)/shard_map/all_to_all | solution.py:52
  27.3 148.1 %all-gather.5.cloned.1.call-start = ((), (), s32[]{:S(2)}) async-start(), calls=%async_computation.3 | async-start | bytes 1179648 | tf_op jit(solution)/shard_map/all_gather | solution.py:84
  103.4 300.4 %all-to-all-start.1 = ((bf16[8,1024,128]{2,0,1:T(8,128)(2,1)}), bf16[8,1024,128]{2,0,1:T(8,128)(2,1)}, u32[]{:S(2)}, u32[]{:S(2)}) async-start(bf16[8,1024,128]{2,0,1:T(8,128)(2,1)} %all-gather.3.cloned.1.call-done), calls=%async_computation.1 | async-start | bytes 4194304 | tf_op jit(solution)/shard_map/all_to_all | solution.py:69
  110.3 278.6 %all-reduce.2.cloned.1.call-start = ((), (), s32[]{:S(2)}) async-start(), calls=%async_computation.4 | async-start | bytes 8388608 | tf_op jit(solution)/shard_map/psum | solution.py:89
  120.8 70.8 %collective-permute-start.1 = (bf16[8,512,128]{2,1,0:T(8,128)(2,1)S(1)}, bf16[8,512,128]{2,1,0:T(8,128)(2,1)}, u32[]{:S(2)}, u32[]{:S(2)}) collective-permute-start(bf16[8,512,128]{2,1,0:T(8,128)(2,1)S(1)} %bitcast.70), channel_id=1, source_target_pairs={{0,1},{1,2},{2,3},{3,4},{4,5},{5,6},{6,7},{7,0},{8,9},{9,10},{10,1... | collective-permute-start | bytes 3145736 | tf_op jit(solution)/shard_map/ppermute | solution.py:16
  179.9 41.3 %copy-start.2 = (bf16[512,128]{1,0:T(8,128)(2,1)S(1)}, bf16[512,128]{1,0:T(8,128)(2,1)}, u32[]{:S(2)}) copy-start(bf16[512,128]{1,0:T(8,128)(2,1)} %param.12) | copy-start | bytes 393220
  179.9 41.3 %copy-start.3 = (f32[3,128]{1,0:T(4,128)S(1)}, f32[3,128]{1,0:T(4,128)}, u32[]{:S(2)}) copy-start(f32[3,128]{1,0:T(4,128)} %param.14) | copy-start | bytes 4612
  179.9 41.4 %copy-start.4 = (s32[512]{0:T(512)S(1)}, s32[512]{0:T(512)}, u32[]{:S(2)}) copy-start(s32[512]{0:T(512)} %param.13) | copy-start | bytes 6148
  180.0 26.9 %collective-permute-start = (bf16[8,512,128]{2,1,0:T(8,128)(2,1)S(1)}, bf16[8,512,128]{2,1,0:T(8,128)(2,1)S(1)}, u32[]{:S(2)}, u32[]{:S(2)}) collective-permute-start(bf16[8,512,128]{2,1,0:T(8,128)(2,1)S(1)} %bitcast.72), channel_id=1, source_target_pairs={{0,7},{1,0},{2,1},{3,2},{4,3},{5,4},{6,5},{7,6},{8,15},{9,8},{10,9... | collective-permute-start | bytes 3145736 | tf_op jit(solution)/shard_map/ppermute | solution.py:18
  191.6 27.6 %collective-permute-start.3 = (bf16[8,512,128]{2,1,0:T(8,128)(2,1)}, bf16[8,512,128]{2,1,0:T(8,128)(2,1)}, u32[]{:S(2)}, u32[]{:S(2)}) collective-permute-start(bf16[8,512,128]{2,1,0:T(8,128)(2,1)} %collective-permute-done.1), channel_id=1, source_target_pairs={{0,1},{1,2},{2,3},{3,4},{4,5},{5,6},{6,7},{7,0},{8,9},{9,10},{10,1... | collective-permute-start | bytes 3145736 | tf_op jit(solution)/shard_map/ppermute | solution.py:16
  206.9 190.0 %collective-permute-start.2 = (bf16[8,512,128]{2,1,0:T(8,128)(2,1)S(1)}, bf16[8,512,128]{2,1,0:T(8,128)(2,1)}, u32[]{:S(2)}, u32[]{:S(2)}) collective-permute-start(bf16[8,512,128]{2,1,0:T(8,128)(2,1)S(1)} %collective-permute-done), channel_id=1, source_target_pairs={{0,7},{1,0},{2,1},{3,2},{4,3},{5,4},{6,5},{7,6},{8,15},{9,8},{10,9... | collective-permute-start | bytes 3145736 | tf_op jit(solution)/shard_map/ppermute | solution.py:18
  219.2 182.4 %collective-permute-start.5 = (bf16[8,512,128]{2,1,0:T(8,128)(2,1)}, bf16[8,512,128]{2,1,0:T(8,128)(2,1)}, u32[]{:S(2)}, u32[]{:S(2)}) collective-permute-start(bf16[8,512,128]{2,1,0:T(8,128)(2,1)} %collective-permute-done.3), channel_id=1, source_target_pairs={{0,1},{1,2},{2,3},{3,4},{4,5},{5,6},{6,7},{7,0},{8,9},{9,10},{10,1... | collective-permute-start | bytes 3145736 | tf_op jit(solution)/shard_map/ppermute | solution.py:16
  396.9 26.0 %collective-permute-start.4 = (bf16[8,512,128]{2,1,0:T(8,128)(2,1)}, bf16[8,512,128]{2,1,0:T(8,128)(2,1)}, u32[]{:S(2)}, u32[]{:S(2)}) collective-permute-start(bf16[8,512,128]{2,1,0:T(8,128)(2,1)} %collective-permute-done.2), channel_id=1, source_target_pairs={{0,7},{1,0},{2,1},{3,2},{4,3},{5,4},{6,5},{7,6},{8,15},{9,8},{10,9... | collective-permute-start | bytes 3145736 | tf_op jit(solution)/shard_map/ppermute | solution.py:18
  401.6 26.6 %collective-permute-start.6 = (bf16[8,512,128]{2,1,0:T(8,128)(2,1)}, bf16[8,512,128]{2,1,0:T(8,128)(2,1)}, u32[]{:S(2)}, u32[]{:S(2)}) collective-permute-start(bf16[8,512,128]{2,1,0:T(8,128)(2,1)} %collective-permute-done.5), channel_id=1, source_target_pairs={{0,1},{1,2},{2,3},{3,4},{4,5},{5,6},{6,7},{7,0},{8,9},{9,10},{10,1... | collective-permute-start | bytes 3145736 | tf_op jit(solution)/shard_map/ppermute | solution.py:16
  412.2 3.2 copy-start.1
Sparse Core Ops, SparseCore 0:
  11.9 91.4 all-gather.2
  105.4 69.9 all-gather.4
  180.1 208.7 all-reduce.1
